TPU v7x, 32 devices: a whole 2x2x4 slice. The times are simulated.
32 devices in a mesh: groups: 2 (over y), frame: 4 (over z), query: 2 (over x), chan: 2 (over core).
Axes of the slice: x: 2, y: 2, z: 4, core: 2. Of those that a mesh axis runs over, the one named last changes fastest.
Arguments:
- features: bfloat16 [8, 64, 64, 256], P(('groups', 'frame'), None, None, 'chan'), parts along dimension 0, may hold values from -6 to 6
- query_frame: int32 [256], P(('groups', 'query')), parts along dimension 0, may hold values from 0 to 3
- query_pixel: int32 [256, 2], P(('groups', 'query')), parts along dimension 0, may hold values from 0 to 63
- conv_first: bfloat16 [3, 3, 1, 16], replicated, may hold values from -2 to 2
- conv_second: bfloat16 [3, 3, 16, 32], replicated, may hold values from -0.5 to 0.5
- depth_kernel: float32 [2, 3, 512], replicated, may hold values from -3 to 3
- w_in: bfloat16 [2, 2048, 512], P(None, ('frame', 'chan')), may hold values from -0.25 to 0.25
- w_out: bfloat16 [2, 2048, 512], P(None, ('frame', 'chan')), may hold values from -0.125 to 0.125
Outputs:
- tracks: bfloat16 [256, 4, 512], P(('groups', 'query'), 'frame'), parts along dimension 0
There are 2 independent parts, one for each index of `groups`. A program takes and returns all parts, laid end to end along the dimension named above; an argument that names none is the same for every part. Nothing has to cross between parts.
All inputs are finite; a program needn't handle non-finite values.
Results may differ from a plain program's by a relative error of at most 0.02.
Values may be sent and summed in bfloat16 or wider, within the bound.
A program may use at most 64 MiB of HBM per device.

v0:
```python
import math
import jax
import jax.numpy as jnp
from jax import lax
from jax.sharding import PartitionSpec as P

MIXERS = 2


def padded_2(block, sides, width):
    for axis, dim in sides:
        count = lax.axis_size(axis)
        forward = [(i, i + 1) for i in range(count - 1)]
        backward = [(target, source) for source, target in forward]
        low = lax.ppermute(
            lax.slice_in_dim(block, block.shape[dim] - width, None, axis=dim), axis, forward
        )
        high = lax.ppermute(lax.slice_in_dim(block, 0, width, axis=dim), axis, backward)
        block = jnp.concatenate([low, block, high], axis=dim)
    return block


def pool_maps(corr_maps, conv_first, conv_second):
    first_maps = lax.conv_general_dilated(
        corr_maps,
        conv_first,
        (2, 2),
        "SAME",
        dimension_numbers=("HWCN", "HWIO", "HWCN"),
        preferred_element_type=jnp.float32,
    )
    first_maps = jax.nn.relu(first_maps).astype(jnp.bfloat16)
    second_maps = lax.conv_general_dilated(
        first_maps,
        conv_second,
        (2, 2),
        "SAME",
        dimension_numbers=("HWCN", "HWIO", "HWCN"),
        preferred_element_type=jnp.float32,
    )
    second_maps = jax.nn.relu(second_maps)
    window = second_maps.shape[0] // 4
    pooled = second_maps.reshape(
        4, window, 4, window, second_maps.shape[2], second_maps.shape[3]
    ).mean(axis=(1, 3))
    return pooled.reshape(16 * second_maps.shape[2], second_maps.shape[3]).T


def layer_norm(state):
    centre = state - jnp.mean(state, axis=-1, keepdims=True)
    spread = jnp.mean(centre * centre, axis=-1, keepdims=True)
    return (centre * lax.rsqrt(spread + 1e-05)).astype(jnp.bfloat16)


def depth_mix(padded, kernel):
    length = padded.shape[1] - 2
    wide = padded.astype(jnp.float32)
    summed = (
        kernel[0] * wide[:, :length] + kernel[1] * wide[:, 1 : length + 1] + kernel[2] * wide[:, 2:]
    )
    return summed.astype(jnp.bfloat16)


def on_device(
    features, query_frame, query_pixel, conv_first, conv_second, depth_kernel, w_in, w_out
):
    frame_count = features.shape[0]
    side_cells = features.shape[1]
    chan_width = features.shape[3]
    row_ids = query_pixel[:, 0]
    col_ids = query_pixel[:, 1]
    local_frame = query_frame - lax.axis_index("frame") * frame_count
    owned_mask = ((local_frame >= 0) & (local_frame < frame_count)).astype(jnp.float32)
    picked = features[jnp.clip(local_frame, 0, frame_count - 1), row_ids, col_ids, :].astype(
        jnp.float32
    )
    picked = picked * owned_mask[:, None]
    query_vectors = lax.psum(picked.astype(jnp.bfloat16), "frame")
    corr_scale = 1.0 / math.sqrt(chan_width * lax.axis_size("chan"))
    flat = features.reshape(frame_count * side_cells * side_cells, chan_width)
    local_corr = jnp.dot(flat, query_vectors.T, preferred_element_type=jnp.float32)
    summed = lax.psum_scatter(
        local_corr.astype(jnp.bfloat16), "chan", scatter_dimension=1, tiled=True
    ).astype(jnp.float32)
    corr_maps = (
        (summed * corr_scale)
        .astype(jnp.bfloat16)
        .reshape(frame_count, side_cells, side_cells, 1, summed.shape[1])
    )
    pooled = lax.map(lambda frame_maps: pool_maps(frame_maps, conv_first, conv_second), corr_maps)
    state = jnp.transpose(pooled, (1, 0, 2))
    for mixer in range(MIXERS):
        normed = layer_norm(state)
        padded = padded_2(normed, (("frame", 1),), 1)
        mixed = depth_mix(padded, depth_kernel[mixer])
        row_block = mixed.reshape(-1, mixed.shape[2])
        empty = jnp.zeros(row_block.shape, jnp.float32)
        in_piece = lax.all_gather(w_in[mixer], ("frame", "chan"), axis=0, tiled=True)
        out_piece = lax.all_gather(w_out[mixer], ("frame", "chan"), axis=0, tiled=True)
        pre_act = lax.dot_general(
            row_block, in_piece, (((1,), (1,)), ((), ())), preferred_element_type=jnp.float32
        )
        hidden = jax.nn.gelu(pre_act, approximate=False).astype(jnp.bfloat16)
        update = empty + jnp.dot(hidden, out_piece, preferred_element_type=jnp.float32)
        state = state + update.reshape(state.shape)
    tracks = state.astype(jnp.bfloat16)
    tracks = lax.all_gather(tracks, "chan", axis=0, tiled=True)
    return tracks


def solution(mesh):
    in_specs = (
        P(("groups", "frame"), None, None, "chan"),
        P(("groups", "query")),
        P(("groups", "query"), None),
        P(),
        P(),
        P(),
        P(None, ("frame", "chan"), None),
        P(None, ("frame", "chan"), None),
    )
    out_specs = P(("groups", "query"), "frame", None)
    return jax.shard_map(
        on_device, mesh=mesh, in_specs=in_specs, out_specs=out_specs, check_vma=False
    )
```

profile of v0, /device:TPU:0, one launch (start us, length us, event | category | flops | bytes accessed | tf_op | source)
XLA Modules:
  0.0 164.9 jit_solution(18240802262996446110)
XLA Ops:
  7.4 0.0 copy-start
  7.4 0.0 copy-start.1
  7.4 0.0 copy-start.2
  7.4 0.0 reduce-scatter.2.cloned.1.call-start
  7.4 0.8 and_convert_fusion
  8.2 0.8 fusion.145
  9.0 0.0 copy-done
  9.0 0.8 gather_fusion
  9.8 0.1 multiply_convert_fusion.3
  9.9 20.5 %psum.7 = bf16[64,128]{1,0:T(8,128)(2,1)S(1)} all-reduce(bf16[64,128]{1,0:T(8,128)(2,1)S(1)} %multiply_convert_fusion.3), channel_id=1, replica_groups=mesh['groups'=2,'frame'=4,'query'=2,'chan'=2] {'frame'}, use_global_device_ids=true, to_apply=%region_0.1 | all-reduce | flops 8192 | bytes 32768 | tf_op jit(solution)/shard_map/psum | solution.py:78
  30.4 1.3 fusion
  31.7 0.0 reduce-scatter.2.cloned.1.call-update
  31.7 0.0 all-gather.10.cloned.1.call-start
  31.8 0.0 copy-done.1
  31.8 0.9 fusion.208
  32.6 0.0 all-gather.10.cloned.1.call-update
  32.6 0.0 all-gather.12.cloned.1.call-start
  32.7 0.0 copy-done.2
  32.7 0.8 fusion.209
  33.6 0.0 all-gather.12.cloned.1.call-update
  33.6 0.0 all-gather.14.cloned.1.call-start
  33.6 0.5 all-gather.14.cloned.1.call-update
  34.2 0.0 all-gather.16.cloned.1.call-start
  34.2 0.0 copy-start.4
  34.2 0.0 copy-start.5
  34.2 0.7 all-gather.16.cloned.1.call-update
  34.9 3.1 %reduce-scatter.2.cloned.1.call-done = bf16[4096,32]{0,1:T(8,128)(2,1)} async-done(((bf16[4096,64]{0,1:T(8,128)(2,1)}), bf16[4096,32]{0,1:T(8,128)(2,1)}) %reduce-scatter.2.cloned.1.call-update) | async-done | bytes 262160 | tf_op jit(solution)/shard_map/reduce_scatter | solution.py:82
  38.0 1.0 multiply_convert_fusion
  39.0 1.3 squeeze.21
  40.4 4.8 %copy.11 = bf16[64,64,1,32]{3,2,1,0:T(2,128)(2,1)S(1)} copy(bf16[64,64,1,32]{1,0,3,2:T(8,128)(2,1)} %squeeze.21) | data formatting | bytes 524288 | tf_op jit(solution)/shard_map/while/body/jit(dynamic_index_in_dim)/squeeze | solution.py:90
  45.1 0.0 copy-done.4
  45.1 0.0 copy-done.5
  45.2 8.0 %fusion.5 = f32[16,16,32,32]{2,3,1,0:T(8,128)} fusion(bf16[3,3,16,32]{3,2,1,0:T(8,128)(2,1)S(1)} %copy-done.4, bf16[64,64,1,32]{3,2,1,0:T(2,128)(2,1)S(1)} %copy.11, bf16[3,3,1,16]{3,1,2,0:T(4,128)(2,1)S(1)} %copy-done.5), kind=kOutput, calls=%fused_computation.7 | convolution fusion | flops 82936832 | bytes 1320224 | tf_op jit(solution)/shard_map/while/body/eval_jaxpr/conv_general_dilated | solution.py:33
  53.2 0.0 copy-start.3
  53.2 2.8 %reduce_sum.46 = f32[4,4,32,32]{2,3,1,0:T(8,128)S(1)} reduce(f32[4,4,4,4,32,32]{4,5,3,2,1,0:T(8,128)} %bitcast.79, f32[]{:T(128)} %constant.16.clone.1), dimensions={1,3}, to_apply=%region_2.3 | reduce | flops 245760 | bytes 1114116 | tf_op jit(solution)/shard_map/while/body/eval_jaxpr/reduce_sum | solution.py:45
  56.0 0.1 fusion.207
  56.1 0.2 copy.13
  56.3 0.2 div.19
  56.5 0.2 multiply_reduce_fusion.1
  56.7 0.1 fusion.117
  56.8 3.6 %collective-permute-start = (bf16[32,1,512]{2,0,1:T(8,128)(2,1)S(1)}, bf16[32,1,512]{2,0,1:T(8,128)(2,1)S(1)}, u32[]{:S(2)}, u32[]{:S(2)}) collective-permute-start(bf16[32,1,512]{2,0,1:T(8,128)(2,1)S(1)} %fusion.117), channel_id=1, source_target_pairs={{0,4},{4,8},{8,12},{1,5},{5,9},{9,13},{2,6},{6,10},{10,14},{3,7},{... | collective-permute-start | bytes 98312 | tf_op jit(solution)/shard_map/ppermute | solution.py:15
  60.4 1.3 collective-permute-start.1
  61.7 0.0 copy-done.3
  61.7 0.2 collective-permute-done
  62.0 4.2 %collective-permute-done.1 = bf16[32,1,512]{2,0,1:T(8,128)(2,1)S(1)} collective-permute-done((bf16[32,1,512]{2,0,1:T(8,128)(2,1)S(1)}, bf16[32,1,512]{2,0,1:T(8,128)(2,1)S(1)}, u32[]{:S(2)}, u32[]{:S(2)}) %collective-permute-start.1) | collective-permute-done | bytes 32800 | tf_op jit(solution)/shard_map/ppermute | solution.py:18
  66.2 0.0 all-gather.10.cloned.1.call-done
  66.2 24.8 %all-gather.12.cloned.1.call-done = bf16[1,2048,512]{2,1,0:T(8,128)(2,1)} async-done(((bf16[1,256,512]{2,1,0:T(8,128)(2,1)}), bf16[1,2048,512]{2,1,0:T(8,128)(2,1)}) %all-gather.12.cloned.1.call-update) | async-done | bytes 2097168 | tf_op jit(solution)/shard_map/all_gather | solution.py:99
  91.0 3.6 %fusion.211 = (f32[32]{0:T(128)S(1)}, f32[32,512]{1,0:T(8,128)S(1)}) fusion(bf16[1,2048,512]{2,1,0:T(8,128)(2,1)} %all-gather.12.cloned.1.call-done, bf16[1,2048,512]{2,1,0:T(8,128)(2,1)} %all-gather.10.cloned.1.call-done, f32[32,3,512]{2,0,1:T(8,128)S(1)} %maximum_convert_fusion.4, f32[512]{0:T(512)S(1)} %bitcast.84, f32[512]{0:T(512)S(1)} %bitcast.85, ...), kind=kOutput, calls=%fused_computation.229 | convolution fusion | flops 138608608 | bytes 4528256 | tf_op jit(solution)/shard_map/dot_general | solution.py:104
  94.6 0.2 multiply_reduce_fusion
  94.8 0.1 fusion.118
  94.9 3.3 %collective-permute-start.2 = (bf16[32,1,512]{2,0,1:T(8,128)(2,1)S(1)}, bf16[32,1,512]{2,0,1:T(8,128)(2,1)S(1)}, u32[]{:S(2)}, u32[]{:S(2)}) collective-permute-start(bf16[32,1,512]{2,0,1:T(8,128)(2,1)S(1)} %fusion.118), channel_id=1, source_target_pairs={{0,4},{4,8},{8,12},{1,5},{5,9},{9,13},{2,6},{6,10},{10,14},{3,7},{... | collective-permute-start | bytes 98312 | tf_op jit(solution)/shard_map/ppermute | solution.py:15
  98.3 1.3 collective-permute-start.3
  99.6 0.3 collective-permute-done.2
  99.8 5.6 %collective-permute-done.3 = bf16[32,1,512]{2,0,1:T(8,128)(2,1)S(1)} collective-permute-done((bf16[32,1,512]{2,0,1:T(8,128)(2,1)S(1)}, bf16[32,1,512]{2,0,1:T(8,128)(2,1)S(1)}, u32[]{:S(2)}, u32[]{:S(2)}) %collective-permute-start.3) | collective-permute-done | bytes 32800 | tf_op jit(solution)/shard_map/ppermute | solution.py:18
  105.5 16.5 %all-gather.14.cloned.1.call-done = bf16[1,2048,512]{2,1,0:T(8,128)(2,1)} async-done(((bf16[1,256,512]{2,1,0:T(8,128)(2,1)}), bf16[1,2048,512]{2,1,0:T(8,128)(2,1)}) %all-gather.14.cloned.1.call-update) | async-done | bytes 2097168 | tf_op jit(solution)/shard_map/all_gather | solution.py:98
  122.0 29.3 %all-gather.16.cloned.1.call-done = bf16[1,2048,512]{2,1,0:T(8,128)(2,1)} async-done(((bf16[1,256,512]{2,1,0:T(8,128)(2,1)}), bf16[1,2048,512]{2,1,0:T(8,128)(2,1)}) %all-gather.16.cloned.1.call-update) | async-done | bytes 2097168 | tf_op jit(solution)/shard_map/all_gather | solution.py:99
  151.3 3.5 %fusion.20 = bf16[32,512]{1,0:T(8,128)(2,1)S(1)} fusion(f32[32,512]{1,0:T(8,128)S(1)} %get-tuple-element.33, bf16[1,2048,512]{2,1,0:T(8,128)(2,1)} %all-gather.16.cloned.1.call-done, bf16[1,2048,512]{2,1,0:T(8,128)(2,1)} %all-gather.14.cloned.1.call-done, f32[32,3,512]{2,0,1:T(8,128)S(1)} %maximum_convert_fusion.5, f32[512]{0:T(512)S(1)} %bitcast.82, ...), kind=kOutput, calls=%fused_computation.18 | convolution fusion | flops 138608640 | bytes 4495360 | tf_op jit(solution)/shard_map/dot_general | solution.py:104
  154.8 1.9 %all-gather.4 = bf16[64,512]{1,0:T(8,128)(2,1)S(1)} all-gather(bf16[32,512]{1,0:T(8,128)(2,1)S(1)} %fusion.20), channel_id=6, replica_groups=mesh['groups'=2,'frame'=4,'query'=2,'chan'=2] {'chan'}, dimensions={0}, use_global_device_ids=true | all-gather | bytes 98304 | tf_op jit(solution)/shard_map/all_gather | solution.py:107
  156.7 0.6 copy.18
  (7 shorter events, 0.1 us)
Async XLA Ops:
  7.4 1.6 copy-start
  7.4 24.4 %copy-start.1 = (bf16[2,256,512]{2,1,0:T(8,128)(2,1)S(1)}, bf16[2,256,512]{2,1,0:T(8,128)(2,1)}, u32[]{:S(2)}) copy-start(bf16[2,256,512]{2,1,0:T(8,128)(2,1)} %param.14) | copy-start | bytes 1572868
  7.4 25.3 %copy-start.2 = (bf16[2,256,512]{2,1,0:T(8,128)(2,1)S(1)}, bf16[2,256,512]{2,1,0:T(8,128)(2,1)}, u32[]{:S(2)}) copy-start(bf16[2,256,512]{2,1,0:T(8,128)(2,1)} %param.15) | copy-start | bytes 1572868
  7.4 30.6 %reduce-scatter.2.cloned.1.call-start = ((), (), s32[]{:S(2)}) async-start(), calls=%async_computation.1 | async-start | bytes 786432 | tf_op jit(solution)/shard_map/reduce_scatter | solution.py:82
  31.7 34.5 %all-gather.10.cloned.1.call-start = ((), (), s32[]{:S(2)}) async-start(), calls=%async_computation.2 | async-start | bytes 2359296 | tf_op jit(solution)/shard_map/all_gather | solution.py:98
  32.6 58.4 %all-gather.12.cloned.1.call-start = ((), (), s32[]{:S(2)}) async-start(), calls=%async_computation.3 | async-start | bytes 2359296 | tf_op jit(solution)/shard_map/all_gather | solution.py:99
  33.6 88.4 %all-gather.14.cloned.1.call-start = ((), (), s32[]{:S(2)}) async-start(), calls=%async_computation.4 | async-start | bytes 2359296 | tf_op jit(solution)/shard_map/all_gather | solution.py:98
  34.2 117.2 %all-gather.16.cloned.1.call-start = ((), (), s32[]{:S(2)}) async-start(), calls=%async_computation.5 | async-start | bytes 2359296 | tf_op jit(solution)/shard_map/all_gather | solution.py:99
  34.2 10.9 %copy-start.4 = (bf16[3,3,16,32]{3,2,1,0:T(8,128)(2,1)S(1)}, bf16[3,3,16,32]{3,2,1,0:T(8,128)(2,1)}, u32[]{:S(2)}) copy-start(bf16[3,3,16,32]{3,2,1,0:T(8,128)(2,1)} %param.12) | copy-start | bytes 27652
  34.2 10.9 %copy-start.5 = (bf16[3,3,1,16]{3,1,2,0:T(4,128)(2,1)S(1)}, bf16[3,3,1,16]{3,1,2,0:T(4,128)(2,1)}, u32[]{:S(2)}) copy-start(bf16[3,3,1,16]{3,1,2,0:T(4,128)(2,1)} %param.11) | copy-start | bytes 868
  53.2 8.5 %copy-start.3 = (f32[2,3,512]{2,0,1:T(2,128)S(1)}, f32[2,3,512]{2,0,1:T(2,128)}, u32[]{:S(2)}) copy-start(f32[2,3,512]{2,0,1:T(2,128)} %param.13) | copy-start | bytes 36868
  56.8 5.2 %collective-permute-start = (bf16[32,1,512]{2,0,1:T(8,128)(2,1)S(1)}, bf16[32,1,512]{2,0,1:T(8,128)(2,1)S(1)}, u32[]{:S(2)}, u32[]{:S(2)}) collective-permute-start(bf16[32,1,512]{2,0,1:T(8,128)(2,1)S(1)} %fusion.117), channel_id=1, source_target_pairs={{0,4},{4,8},{8,12},{1,5},{5,9},{9,13},{2,6},{6,10},{10,14},{3,7},{... | collective-permute-start | bytes 98312 | tf_op jit(solution)/shard_map/ppermute | solution.py:15
  60.4 5.8 %collective-permute-start.1 = (bf16[32,1,512]{2,0,1:T(8,128)(2,1)S(1)}, bf16[32,1,512]{2,0,1:T(8,128)(2,1)S(1)}, u32[]{:S(2)}, u32[]{:S(2)}) collective-permute-start(bf16[32,1,512]{2,0,1:T(8,128)(2,1)S(1)} %fusion.117), channel_id=1, source_target_pairs={{4,0},{8,4},{12,8},{5,1},{9,5},{13,9},{6,2},{10,6},{14,10},{7,3},{... | collective-permute-start | bytes 98312 | tf_op jit(solution)/shard_map/ppermute | solution.py:18
  94.9 4.9 %collective-permute-start.2 = (bf16[32,1,512]{2,0,1:T(8,128)(2,1)S(1)}, bf16[32,1,512]{2,0,1:T(8,128)(2,1)S(1)}, u32[]{:S(2)}, u32[]{:S(2)}) collective-permute-start(bf16[32,1,512]{2,0,1:T(8,128)(2,1)S(1)} %fusion.118), channel_id=1, source_target_pairs={{0,4},{4,8},{8,12},{1,5},{5,9},{9,13},{2,6},{6,10},{10,14},{3,7},{... | collective-permute-start | bytes 98312 | tf_op jit(solution)/shard_map/ppermute | solution.py:15
  98.3 7.2 %collective-permute-start.3 = (bf16[32,1,512]{2,0,1:T(8,128)(2,1)S(1)}, bf16[32,1,512]{2,0,1:T(8,128)(2,1)S(1)}, u32[]{:S(2)}, u32[]{:S(2)}) collective-permute-start(bf16[32,1,512]{2,0,1:T(8,128)(2,1)S(1)} %fusion.118), channel_id=1, source_target_pairs={{4,0},{8,4},{12,8},{5,1},{9,5},{13,9},{6,2},{10,6},{14,10},{7,3},{... | collective-permute-start | bytes 98312 | tf_op jit(solution)/shard_map/ppermute | solution.py:18
Sparse Core Ops, SparseCore 0:
  31.8 6.1 reduce-scatter.1
Sparse Core Ops, SparseCore 1:
  33.8 27.3 all-gather.9
  62.6 28.4 all-gather.11
  92.5 29.5 all-gather.13
  123.6 27.6 all-gather.15
where the time goes:
time: 165 us
  waiting for transfers between devices  85.4 us (52%)
  blocking collectives  22.4 us (14%)
  matrix products  16.4 us (10%)
  between operations  15.3 us (9%)
  local copies, waits for them, and re-layouts  9.7 us (6%)
  starting transfers between devices  9.66 us (6%)
  other arithmetic  6.17 us (4%)
    all_gather x2, waiting for transfers between devices, on_device(): lax.all_gather(w_out[mixer], ('frame', 'chan'), axis=0, tiled=True)  54.1 us
    psum x1, blocking collectives, on_device(): query_vectors = lax.psum(picked.astype(jnp.bfloat16), 'frame')  20.5 us
    all_gather x2, waiting for transfers between devices, on_device(): lax.all_gather(w_in[mixer], ('frame', 'chan'), axis=0, tiled=True)  16.6 us
    ppermute x2, waiting for transfers between devices, padded_2(): lax.ppermute(lax.slice_in_dim(block, 0, width, axis=dim), axis, backward)  9.86 us
    conv_general_dilated x1, matrix products, pool_maps(): lax.conv_general_dilated(first_maps, conv_second, (2, 2), 'SAME', dimensi...  8.04 us
    dot_general x2, matrix products, on_device(): jnp.dot(hidden, out_piece, preferred_element_type=jnp.float32)  7.08 us
    ppermute x2, starting transfers between devices, padded_2(): lax.ppermute(lax.slice_in_dim(block, block.shape[dim] - width, None, axis...  6.9 us
    squeeze x2, local copies, waits for them, and re-layouts, on_device(): lax.map(lambda frame_maps: pool_maps(frame_maps, conv_first, conv_second)...  6.11 us
  transfers between devices with their start and end apart: 9, of which 8 were waited for; matrix products, arithmetic and copies ran while one was open for 15% of the time, Pallas kernels for 0%

commit v1 on v0

--- a/solution.py
+++ b/solution.py
@@ -95,7 +95,12 @@
         mixed = depth_mix(padded, depth_kernel[mixer])
         row_block = mixed.reshape(-1, mixed.shape[2])
         empty = jnp.zeros(row_block.shape, jnp.float32)
-        in_piece = lax.all_gather(w_in[mixer], ("frame", "chan"), axis=0, tiled=True)
+        in_piece = jnp.concatenate(
+            lax.all_to_all(
+                jnp.stack([w_in[mixer]] * lax.axis_size(("frame", "chan"))), ("frame", "chan"), 0, 0
+            ),
+            axis=0,
+        )
         out_piece = lax.all_gather(w_out[mixer], ("frame", "chan"), axis=0, tiled=True)
         pre_act = lax.dot_general(
             row_block, in_piece, (((1,), (1,)), ((), ())), preferred_element_type=jnp.float32

time: 165 us -> 202 us (1.22)
  starting transfers between devices: 9.66 us -> 31.1 us
  waiting for transfers between devices: 85.4 us -> 98.6 us
  local copies, waits for them, and re-layouts: 9.7 us -> 12.4 us
    all_to_all x0 -> x2, waiting for transfers between devices: none -> 82.1 us  [on_device(): lax.all_to_all(jnp.stack([w_in[mixer]] * lax.axis_size(('frame', 'chan'))...]
    all_gather x2, waiting for transfers between devices: 54.1 us -> 0.05 us  [on_device(): lax.all_gather(w_out[mixer], ('frame', 'chan'), axis=0, tiled=True)]
    all_gather x2 -> x0, waiting for transfers between devices: 16.6 us -> none  [on_device(): lax.all_gather(w_in[mixer], ('frame', 'chan'), axis=0, tiled=True)]
    ppermute x2, starting transfers between devices: 6.9 us -> 20.4 us  [padded_2(): lax.ppermute(lax.slice_in_dim(block, block.shape[dim] - width, None, axis...]
    ppermute x2, waiting for transfers between devices: 0.53 us -> 11.7 us  [padded_2(): lax.ppermute(lax.slice_in_dim(block, block.shape[dim] - width, None, axis...]
    all_to_all x0 -> x2, starting transfers between devices: none -> 7.98 us  [on_device(): lax.all_to_all(jnp.stack([w_in[mixer]] * lax.axis_size(('frame', 'chan'))...]
    ppermute x2, waiting for transfers between devices: 9.86 us -> 4.23 us  [padded_2(): lax.ppermute(lax.slice_in_dim(block, 0, width, axis=dim), axis, backward)]
    another operation x0 -> x2, local copies, waits for them, and re-layouts: none -> 3.19 us  [on_device(): jnp.stack([w_in[mixer]] * lax.axis_size(('frame', 'chan')))]
  transfers between devices with their start and end apart: 9 -> 9, of which waited for: 8 -> 4; matrix products, arithmetic and copies ran while one was open for 15% -> 13% of each run, Pallas kernels for 0% -> 0%
where the time goes in v1:
time: 202 us
  waiting for transfers between devices  98.6 us (49%)
  starting transfers between devices  31.1 us (15%)
  blocking collectives  22.4 us (11%)
  matrix products  15.8 us (8%)
  between operations  15.1 us (7%)
  local copies, waits for them, and re-layouts  12.4 us (6%)
  other arithmetic  6.25 us (3%)
    all_to_all x2, waiting for transfers between devices, on_device(): lax.all_to_all(jnp.stack([w_in[mixer]] * lax.axis_size(('frame', 'chan'))...  82.1 us
    psum x1, blocking collectives, on_device(): query_vectors = lax.psum(picked.astype(jnp.bfloat16), 'frame')  20.5 us
    ppermute x2, starting transfers between devices, padded_2(): lax.ppermute(lax.slice_in_dim(block, block.shape[dim] - width, None, axis...  20.4 us
    ppermute x2, waiting for transfers between devices, padded_2(): lax.ppermute(lax.slice_in_dim(block, block.shape[dim] - width, None, axis...  11.7 us
    conv_general_dilated x1, matrix products, pool_maps(): lax.conv_general_dilated(first_maps, conv_second, (2, 2), 'SAME', dimensi...  8.04 us
    all_to_all x2, starting transfers between devices, on_device(): lax.all_to_all(jnp.stack([w_in[mixer]] * lax.axis_size(('frame', 'chan'))...  7.98 us
    dot_general x2, matrix products, on_device(): jnp.dot(hidden, out_piece, preferred_element_type=jnp.float32)  6.46 us
    squeeze x2, local copies, waits for them, and re-layouts, on_device(): lax.map(lambda frame_maps: pool_maps(frame_maps, conv_first, conv_second)...  6.11 us
  transfers between devices with their start and end apart: 9, of which 4 were waited for; matrix products, arithmetic and copies ran while one was open for 13% of the time, Pallas kernels for 0%

profile of v1, /device:TPU:0, one launch (start us, length us, event | category | flops | bytes accessed | tf_op | source)
XLA Modules:
  0.0 201.6 jit_solution(2781545342387816600)
XLA Ops:
  7.4 0.0 copy-start
  7.4 0.0 copy-start.3
  7.4 0.0 copy-start.4
  7.4 0.0 reduce-scatter.2.cloned.1.call-start
  7.4 0.8 and_convert_fusion
  8.2 0.8 fusion.143
  9.0 0.0 copy-done
  9.0 0.8 gather_fusion
  9.8 0.1 multiply_convert_fusion.3
  9.9 20.5 %psum.7 = bf16[64,128]{1,0:T(8,128)(2,1)S(1)} all-reduce(bf16[64,128]{1,0:T(8,128)(2,1)S(1)} %multiply_convert_fusion.3), channel_id=1, replica_groups=mesh['groups'=2,'frame'=4,'query'=2,'chan'=2] {'frame'}, use_global_device_ids=true, to_apply=%region_0.1 | all-reduce | flops 8192 | bytes 32768 | tf_op jit(solution)/shard_map/psum | solution.py:78
  30.4 1.3 fusion
  31.7 0.0 reduce-scatter.2.cloned.1.call-update
  31.7 0.0 all-gather.6.cloned.1.call-start
  31.8 0.0 copy-done.3
  31.8 0.8 fusion.206
  32.6 0.0 all-gather.6.cloned.1.call-update
  32.6 0.0 copy-done.4
  32.7 1.5 stack.6
  34.2 3.6 %all-to-all-start = ((bf16[8,256,512]{2,1,0:T(8,128)(2,1)}), bf16[8,256,512]{2,1,0:T(8,128)(2,1)S(1)}, u32[]{:S(2)}, u32[]{:S(2)}) async-start(bf16[8,256,512]{2,1,0:T(8,128)(2,1)} %stack.6), calls=%async_computation.1 | async-start | bytes 4194304 | tf_op jit(solution)/shard_map/all_to_all | solution.py:99
  37.8 0.0 all-gather.8.cloned.1.call-start
  37.9 0.5 all-gather.8.cloned.1.call-update
  38.4 82.1 %all-to-all-done = bf16[8,256,512]{2,1,0:T(8,128)(2,1)S(1)} async-done(((bf16[8,256,512]{2,1,0:T(8,128)(2,1)}), bf16[8,256,512]{2,1,0:T(8,128)(2,1)S(1)}, u32[]{:S(2)}, u32[]{:S(2)}) %all-to-all-start) | async-done | bytes 2097184 | tf_op jit(solution)/shard_map/all_to_all | solution.py:99
  120.5 0.0 copy-start.1
  120.5 1.7 stack.7
  122.2 0.3 copy-done.1
  122.5 4.4 %all-to-all-start.1 = ((bf16[8,256,512]{2,1,0:T(8,128)(2,1)}), bf16[8,256,512]{2,1,0:T(8,128)(2,1)}, u32[]{:S(2)}, u32[]{:S(2)}) async-start(bf16[8,256,512]{2,1,0:T(8,128)(2,1)} %stack.7), calls=%async_computation.2 | async-start | bytes 4194304 | tf_op jit(solution)/shard_map/all_to_all | solution.py:99
  126.9 0.0 copy-start.6
  126.9 0.0 copy-start.7
  126.9 0.0 reduce-scatter.2.cloned.1.call-done
  127.0 1.0 multiply_convert_fusion
  127.9 1.3 squeeze.15
  129.3 4.8 %copy.11 = bf16[64,64,1,32]{3,2,1,0:T(2,128)(2,1)S(1)} copy(bf16[64,64,1,32]{1,0,3,2:T(8,128)(2,1)} %squeeze.15) | data formatting | bytes 524288 | tf_op jit(solution)/shard_map/while/body/jit(dynamic_index_in_dim)/squeeze | solution.py:90
  134.1 0.0 copy-done.6
  134.1 0.0 copy-done.7
  134.1 8.0 %fusion.5 = f32[16,16,32,32]{2,3,1,0:T(8,128)} fusion(bf16[3,3,16,32]{3,2,1,0:T(8,128)(2,1)S(1)} %copy-done.6, bf16[64,64,1,32]{3,2,1,0:T(2,128)(2,1)S(1)} %copy.11, bf16[3,3,1,16]{3,1,2,0:T(4,128)(2,1)S(1)} %copy-done.7), kind=kOutput, calls=%fused_computation.7 | convolution fusion | flops 82936832 | bytes 1320224 | tf_op jit(solution)/shard_map/while/body/eval_jaxpr/conv_general_dilated | solution.py:33
  142.1 0.0 copy-start.5
  142.1 0.0 copy-start.2
  142.1 2.9 %reduce_sum.46 = f32[4,4,32,32]{2,3,1,0:T(8,128)S(1)} reduce(f32[4,4,4,4,32,32]{4,5,3,2,1,0:T(8,128)} %bitcast.77, f32[]{:T(128)} %constant.16.clone.1), dimensions={1,3}, to_apply=%region_2.3 | reduce | flops 245760 | bytes 1114116 | tf_op jit(solution)/shard_map/while/body/eval_jaxpr/reduce_sum | solution.py:45
  145.0 0.1 fusion.205
  145.2 0.2 copy.13
  145.3 0.2 div.19
  145.5 0.2 multiply_reduce_fusion.1
  145.7 0.1 fusion.107
  145.8 3.8 %collective-permute-start = (bf16[32,1,512]{2,0,1:T(8,128)(2,1)S(1)}, bf16[32,1,512]{2,0,1:T(8,128)(2,1)S(1)}, u32[]{:S(2)}, u32[]{:S(2)}) collective-permute-start(bf16[32,1,512]{2,0,1:T(8,128)(2,1)S(1)} %fusion.107), channel_id=1, source_target_pairs={{0,4},{4,8},{8,12},{1,5},{5,9},{9,13},{2,6},{6,10},{10,14},{3,7},{... | collective-permute-start | bytes 98312 | tf_op jit(solution)/shard_map/ppermute | solution.py:15
  149.6 1.3 collective-permute-start.1
  150.9 0.0 copy-done.5
  150.9 11.4 %collective-permute-done = bf16[32,1,512]{2,0,1:T(8,128)(2,1)S(1)} collective-permute-done((bf16[32,1,512]{2,0,1:T(8,128)(2,1)S(1)}, bf16[32,1,512]{2,0,1:T(8,128)(2,1)S(1)}, u32[]{:S(2)}, u32[]{:S(2)}) %collective-permute-start) | collective-permute-done | bytes 32800 | tf_op jit(solution)/shard_map/ppermute | solution.py:15
  162.4 0.0 collective-permute-done.1
  162.4 0.0 all-gather.6.cloned.1.call-done
  162.4 0.0 copy-done.2
  162.4 3.0 %fusion.208 = (f32[32]{0:T(128)S(1)}, f32[32,512]{1,0:T(8,128)S(1)}) fusion(bf16[1,2048,512]{2,1,0:T(8,128)(2,1)} %all-gather.6.cloned.1.call-done, bf16[2048,512]{1,0:T(8,128)(2,1)S(1)} %bitcast.78, f32[32,3,512]{2,0,1:T(8,128)S(1)} %maximum_convert_fusion.4, f32[512]{0:T(512)S(1)} %bitcast.83, f32[512]{0:T(512)S(1)} %bitcast.84, f32[512]{0:T(512)S(1)} %bitcast.85, ...), kind=kOutput, calls=%fused_computation.228 | convolution fusion | flops 138608608 | bytes 4528256 | tf_op jit(solution)/shard_map/dot_general | solution.py:109
  165.4 0.2 multiply_reduce_fusion
  165.6 0.1 fusion.108
  165.7 16.6 %collective-permute-start.2 = (bf16[32,1,512]{2,0,1:T(8,128)(2,1)S(1)}, bf16[32,1,512]{2,0,1:T(8,128)(2,1)S(1)}, u32[]{:S(2)}, u32[]{:S(2)}) collective-permute-start(bf16[32,1,512]{2,0,1:T(8,128)(2,1)S(1)} %fusion.108), channel_id=1, source_target_pairs={{0,4},{4,8},{8,12},{1,5},{5,9},{9,13},{2,6},{6,10},{10,14},{3,7},{... | collective-permute-start | bytes 98312 | tf_op jit(solution)/shard_map/ppermute | solution.py:15
  182.3 1.3 collective-permute-start.3
  183.6 0.3 collective-permute-done.2
  183.9 4.2 %collective-permute-done.3 = bf16[32,1,512]{2,0,1:T(8,128)(2,1)S(1)} collective-permute-done((bf16[32,1,512]{2,0,1:T(8,128)(2,1)S(1)}, bf16[32,1,512]{2,0,1:T(8,128)(2,1)S(1)}, u32[]{:S(2)}, u32[]{:S(2)}) %collective-permute-start.3) | collective-permute-done | bytes 32800 | tf_op jit(solution)/shard_map/ppermute | solution.py:18
  188.2 0.0 all-to-all-done.1
  188.2 0.0 all-gather.8.cloned.1.call-done
  188.2 3.5 %fusion.16 = bf16[32,512]{1,0:T(8,128)(2,1)S(1)} fusion(f32[32,512]{1,0:T(8,128)S(1)} %get-tuple-element.33, bf16[1,2048,512]{2,1,0:T(8,128)(2,1)} %all-gather.8.cloned.1.call-done, bf16[2048,512]{1,0:T(8,128)(2,1)} %bitcast.20, f32[32,3,512]{2,0,1:T(8,128)S(1)} %maximum_convert_fusion.5, f32[512]{0:T(512)S(1)} %bitcast.81, f32[512]{0:T(512)S(1)} %bitcast.82, ...), kind=kOutput, calls=%fused_computation.14 | convolution fusion | flops 138608640 | bytes 4495360 | tf_op jit(solution)/shard_map/dot_general | solution.py:109
  191.7 1.9 all-gather.2
  193.6 0.6 copy.18
  (8 shorter events, 0.1 us)
Async XLA Ops:
  7.4 1.6 copy-start
  7.4 24.4 %copy-start.3 = (bf16[2,256,512]{2,1,0:T(8,128)(2,1)S(1)}, bf16[2,256,512]{2,1,0:T(8,128)(2,1)}, u32[]{:S(2)}) copy-start(bf16[2,256,512]{2,1,0:T(8,128)(2,1)} %param.15) | copy-start | bytes 1572868
  7.4 25.3 %copy-start.4 = (bf16[2,256,512]{2,1,0:T(8,128)(2,1)S(1)}, bf16[2,256,512]{2,1,0:T(8,128)(2,1)}, u32[]{:S(2)}) copy-start(bf16[2,256,512]{2,1,0:T(8,128)(2,1)} %param.14) | copy-start | bytes 1572868
  7.4 119.6 %reduce-scatter.2.cloned.1.call-start = ((), (), s32[]{:S(2)}) async-start(), calls=%async_computation.3 | async-start | bytes 786432 | tf_op jit(solution)/shard_map/reduce_scatter | solution.py:82
  31.7 130.7 %all-gather.6.cloned.1.call-start = ((), (), s32[]{:S(2)}) async-start(), calls=%async_computation.4 | async-start | bytes 2359296 | tf_op jit(solution)/shard_map/all_gather | solution.py:104
  34.2 86.3 %all-to-all-start = ((bf16[8,256,512]{2,1,0:T(8,128)(2,1)}), bf16[8,256,512]{2,1,0:T(8,128)(2,1)S(1)}, u32[]{:S(2)}, u32[]{:S(2)}) async-start(bf16[8,256,512]{2,1,0:T(8,128)(2,1)} %stack.6), calls=%async_computation.1 | async-start | bytes 4194304 | tf_op jit(solution)/shard_map/all_to_all | solution.py:99
  37.8 150.4 %all-gather.8.cloned.1.call-start = ((), (), s32[]{:S(2)}) async-start(), calls=%async_computation.5 | async-start | bytes 2359296 | tf_op jit(solution)/shard_map/all_gather | solution.py:104
  120.5 2.0 %copy-start.1 = (bf16[8,256,512]{2,1,0:T(8,128)(2,1)}, bf16[8,256,512]{2,1,0:T(8,128)(2,1)S(1)}, u32[]{:S(2)}) copy-start(bf16[8,256,512]{2,1,0:T(8,128)(2,1)S(1)} %all-to-all-done) | copy-start | bytes 6291460
  122.5 65.7 %all-to-all-start.1 = ((bf16[8,256,512]{2,1,0:T(8,128)(2,1)}), bf16[8,256,512]{2,1,0:T(8,128)(2,1)}, u32[]{:S(2)}, u32[]{:S(2)}) async-start(bf16[8,256,512]{2,1,0:T(8,128)(2,1)} %stack.7), calls=%async_computation.2 | async-start | bytes 4194304 | tf_op jit(solution)/shard_map/all_to_all | solution.py:99
  126.9 7.2 %copy-start.6 = (bf16[3,3,16,32]{3,2,1,0:T(8,128)(2,1)S(1)}, bf16[3,3,16,32]{3,2,1,0:T(8,128)(2,1)}, u32[]{:S(2)}) copy-start(bf16[3,3,16,32]{3,2,1,0:T(8,128)(2,1)} %param.12) | copy-start | bytes 27652
  126.9 7.2 %copy-start.7 = (bf16[3,3,1,16]{3,1,2,0:T(4,128)(2,1)S(1)}, bf16[3,3,1,16]{3,1,2,0:T(4,128)(2,1)}, u32[]{:S(2)}) copy-start(bf16[3,3,1,16]{3,1,2,0:T(4,128)(2,1)} %param.11) | copy-start | bytes 868
  142.1 8.8 %copy-start.5 = (f32[2,3,512]{2,0,1:T(2,128)S(1)}, f32[2,3,512]{2,0,1:T(2,128)}, u32[]{:S(2)}) copy-start(f32[2,3,512]{2,0,1:T(2,128)} %param.13) | copy-start | bytes 36868
  142.1 20.3 %copy-start.2 = (bf16[8,256,512]{2,1,0:T(8,128)(2,1)S(1)}, bf16[8,256,512]{2,1,0:T(8,128)(2,1)}, u32[]{:S(2)}) copy-start(bf16[8,256,512]{2,1,0:T(8,128)(2,1)} %copy-done.1) | copy-start | bytes 6291460
  145.8 16.5 %collective-permute-start = (bf16[32,1,512]{2,0,1:T(8,128)(2,1)S(1)}, bf16[32,1,512]{2,0,1:T(8,128)(2,1)S(1)}, u32[]{:S(2)}, u32[]{:S(2)}) collective-permute-start(bf16[32,1,512]{2,0,1:T(8,128)(2,1)S(1)} %fusion.107), channel_id=1, source_target_pairs={{0,4},{4,8},{8,12},{1,5},{5,9},{9,13},{2,6},{6,10},{10,14},{3,7},{... | collective-permute-start | bytes 98312 | tf_op jit(solution)/shard_map/ppermute | solution.py:15
  149.6 12.8 %collective-permute-start.1 = (bf16[32,1,512]{2,0,1:T(8,128)(2,1)S(1)}, bf16[32,1,512]{2,0,1:T(8,128)(2,1)S(1)}, u32[]{:S(2)}, u32[]{:S(2)}) collective-permute-start(bf16[32,1,512]{2,0,1:T(8,128)(2,1)S(1)} %fusion.107), channel_id=1, source_target_pairs={{4,0},{8,4},{12,8},{5,1},{9,5},{13,9},{6,2},{10,6},{14,10},{7,3},{... | collective-permute-start | bytes 98312 | tf_op jit(solution)/shard_map/ppermute | solution.py:18
  165.7 18.2 %collective-permute-start.2 = (bf16[32,1,512]{2,0,1:T(8,128)(2,1)S(1)}, bf16[32,1,512]{2,0,1:T(8,128)(2,1)S(1)}, u32[]{:S(2)}, u32[]{:S(2)}) collective-permute-start(bf16[32,1,512]{2,0,1:T(8,128)(2,1)S(1)} %fusion.108), channel_id=1, source_target_pairs={{0,4},{4,8},{8,12},{1,5},{5,9},{9,13},{2,6},{6,10},{10,14},{3,7},{... | collective-permute-start | bytes 98312 | tf_op jit(solution)/shard_map/ppermute | solution.py:15
  182.3 5.8 %collective-permute-start.3 = (bf16[32,1,512]{2,0,1:T(8,128)(2,1)S(1)}, bf16[32,1,512]{2,0,1:T(8,128)(2,1)S(1)}, u32[]{:S(2)}, u32[]{:S(2)}) collective-permute-start(bf16[32,1,512]{2,0,1:T(8,128)(2,1)S(1)} %fusion.108), channel_id=1, source_target_pairs={{4,0},{8,4},{12,8},{5,1},{9,5},{13,9},{6,2},{10,6},{14,10},{7,3},{... | collective-permute-start | bytes 98312 | tf_op jit(solution)/shard_map/ppermute | solution.py:18
Sparse Core Ops, SparseCore 0:
  31.8 6.1 reduce-scatter.1
Sparse Core Ops, SparseCore 1:
  33.8 44.3 all-gather.5
  79.6 42.0 all-gather.7
